TPU v7x, 32 devices: a whole 2x2x4 slice. The times are simulated.
32 devices in a mesh: row: 8 (over y, x, core), col: 4 (over z).
Axes of the slice: x: 2, y: 2, z: 4, core: 2. Of those that a mesh axis runs over, the one named last changes fastest.
Arguments:
- tokens: bfloat16 [128, 96, 768], P('row', 'col'), as said below
- dw_kernel: float32 [7, 7, 768], replicated, may hold values from -0.875 to 0.875
- norm_gain: float32 [768], replicated, may hold values from 0.5 to 1.5
- norm_shift: float32 [768], replicated, may hold values from -3 to 3
- w_in: bfloat16 [768, 3072], P(None, 'col'), may hold values from -0.21875 to 0.21875
- w_out: bfloat16 [3072, 768], P('col'), may hold values from -0.109375 to 0.109375
- w_kv: bfloat16 [768, 1536], P(None, 'col'), as said below
- queries: bfloat16 [512, 768], replicated, may hold values from -300 to 300, as said below
- latent_gain: float32 [768], replicated, may hold values from 0.5 to 1.5
- w_o: bfloat16 [768, 768], P(None, 'col'), may hold values from -0.21875 to 0.21875
Outputs:
- token_map: bfloat16 [128, 96, 768], P('row', 'col')
- latents: bfloat16 [512, 768], replicated
Inputs may be any that keep to these rules, and one draw needn't show every extreme that they name: Latent queries; a few rows may be far larger than the others. `tokens`: patch token features, roughly unit normal, between -24 and 24; a few cells hold 24 in two channels. `w_kv`: key and value projection weights.
All inputs are finite; a program needn't handle non-finite values.
Results may differ from a plain program's by a relative error of at most 0.011.
Values may be sent and summed in bfloat16 or wider, within the bound.
A program may use at most 64 MiB of HBM per device.

v0:
```python
import math

import jax
import jax.numpy as jnp
from jax import lax
from jax.sharding import PartitionSpec as P

HEADS = 12
HEAD = 64


def with_halo(cells, sides, width):
    for axis, dim in sides:
        count = lax.axis_size(axis)
        ends = count - 1
        head = lax.slice_in_dim(cells, 0, width, axis=dim)
        tail = lax.slice_in_dim(cells, cells.shape[dim] - width, cells.shape[dim], axis=dim)
        cells = jnp.concatenate(
            [
                lax.ppermute(tail, axis, [(i, (i + 1) % count) for i in range(ends)]),
                cells,
                lax.ppermute(head, axis, [((i + 1) % count, i) for i in range(ends)]),
            ],
            axis=dim,
        )
    return cells


def conv_taps(padded, height, width, dw_kernel):
    mixed = jnp.zeros((height, width, padded.shape[2]), jnp.float32)
    for row_tap in range(7):
        for col_tap in range(7):
            mixed = (
                mixed
                + padded[row_tap : row_tap + height, col_tap : col_tap + width]
                * dw_kernel[row_tap, col_tap]
            )
    return mixed


def layer_norm(mixed, norm_gain, norm_shift):
    center = mixed - jnp.mean(mixed, axis=-1, keepdims=True)
    spread = jnp.mean(center * center, axis=-1, keepdims=True)
    return (center * lax.rsqrt(spread + 1e-06) * norm_gain + norm_shift).astype(jnp.bfloat16)


def finish_latents(numer, denom, latent_gain, w_full):
    attended = (numer / denom[..., None]).reshape(numer.shape[0], -1)
    squares = jnp.mean(attended * attended, axis=-1, keepdims=True)
    scaled = (attended * lax.rsqrt(squares + 1e-06) * latent_gain).astype(jnp.bfloat16)
    return jnp.dot(scaled, w_full, preferred_element_type=jnp.float32).astype(jnp.bfloat16)


def body(tokens, dw_kernel, norm_gain, norm_shift, w_in, w_out, w_kv, queries, latent_gain, w_o):
    height, width, width_d = tokens.shape
    latent_count = queries.shape[0]
    padded = with_halo(tokens, (("row", 0), ("col", 1)), 3)
    mixed = conv_taps(padded.astype(jnp.float32), height, width, dw_kernel)
    normed = layer_norm(mixed, norm_gain, norm_shift).reshape(height * width, width_d)
    residual = tokens.reshape(height * width, width_d).astype(jnp.float32)
    hidden = jax.nn.gelu(
        jnp.dot(
            normed,
            lax.all_gather(w_in, "col", axis=1, tiled=True),
            preferred_element_type=jnp.float32,
        )
    ).astype(jnp.bfloat16)
    update = jnp.dot(
        hidden, lax.all_gather(w_out, "col", axis=0, tiled=True), preferred_element_type=jnp.float32
    )
    token_rows = (residual + update).astype(jnp.bfloat16)
    token_map = token_rows.reshape(height, width, width_d)
    keys_vals = jnp.dot(
        token_rows,
        lax.all_gather(w_kv, "col", axis=1, tiled=True),
        preferred_element_type=jnp.float32,
    ).astype(jnp.bfloat16)
    w_full = lax.all_gather(w_o, "col", axis=1, tiled=True)
    key_heads = keys_vals[:, :width_d].reshape(-1, HEADS, HEAD)
    val_heads = keys_vals[:, width_d:].reshape(-1, HEADS, HEAD)
    query_heads = queries.reshape(latent_count, HEADS, HEAD)
    score_scale = 1.0 / math.sqrt(HEAD)
    group_size = math.gcd(HEADS, 4)
    max_parts, den_parts, num_parts = ([], [], [])
    for first_head in range(0, HEADS, group_size):
        scores = (
            jnp.einsum(
                "lhd,thd->lht",
                query_heads[:, first_head : first_head + group_size],
                key_heads[:, first_head : first_head + group_size],
                preferred_element_type=jnp.float32,
            )
            * score_scale
        )
        local_max = jnp.max(scores, axis=-1)
        weights = jnp.exp(scores - local_max[..., None])
        den_parts.append(jnp.sum(weights, axis=-1))
        max_parts.append(local_max)
        num_parts.append(
            jnp.einsum(
                "lht,thd->lhd",
                weights.astype(jnp.bfloat16),
                val_heads[:, first_head : first_head + group_size],
                preferred_element_type=jnp.float32,
            )
        )
    maxima = jnp.concatenate(max_parts, axis=1)
    denom = jnp.concatenate(den_parts, axis=1)
    numer = jnp.concatenate(num_parts, axis=1)
    peak = lax.pmax(maxima, ("row", "col"))
    factor = jnp.exp(maxima - peak)
    den_terms = denom * factor
    num_terms = (numer * factor[..., None]).reshape(latent_count, width_d)
    den_part, num_part = (
        lax.psum_scatter(den_terms, "col", scatter_dimension=0, tiled=True),
        lax.psum_scatter(num_terms, "col", scatter_dimension=0, tiled=True),
    )
    den_share, num_share = lax.psum((den_part, num_part), "row")
    own_rows = finish_latents(
        num_share.reshape(num_share.shape[0], HEADS, HEAD), den_share, latent_gain, w_full
    )
    latents = lax.all_gather(own_rows, "col", axis=0, tiled=True)
    return (token_map, latents)


def solution(mesh):
    in_specs = (
        P("row", "col", None),
        P(),
        P(),
        P(),
        P(None, "col"),
        P("col", None),
        P(None, "col"),
        P(),
        P(),
        P(None, "col"),
    )
    out_specs = (P("row", "col", None), P())
    return jax.shard_map(body, mesh=mesh, in_specs=in_specs, out_specs=out_specs, check_vma=False)
```

profile of v0, /device:TPU:0, one launch (start us, length us, event | category | flops | bytes accessed | tf_op | source)
XLA Modules:
  0.0 479.7 jit_solution(5248755326156885472)
XLA Ops:
  7.2 0.7 all-gather.5.cloned.1.call-update
  8.0 0.7 all-gather.7.cloned.1.call-update
  8.8 2.4 collective-permute-start
  11.2 1.3 collective-permute-start.1
  12.6 0.2 slice_reduce_fusion.47
  12.7 1.2 copy.24
  13.9 0.2 slice_reduce_fusion.48
  14.1 2.3 collective-permute-done.1
  16.5 0.1 fusion.112
  16.6 3.5 collective-permute-start.2
  20.1 1.3 collective-permute-start.3
  21.5 4.3 collective-permute-done.2
  25.8 7.4 %collective-permute-done.3 = bf16[22,3,768]{2,1,0:T(4,128)(2,1)S(1)} collective-permute-done((bf16[22,3,768]{2,1,0:T(4,128)(2,1)S(1)}, bf16[22,3,768]{2,1,0:T(4,128)(2,1)S(1)}, u32[]{:S(2)}, u32[]{:S(2)}) %collective-permute-start.3) | collective-permute-done | bytes 101408 | tf_op jit(solution)/shard_map/ppermute | solution.py:22
  33.2 0.4 maximum_convert_fusion
  33.6 12.3 %fusion.109 = (f32[16,24]{1,0:T(8,128)S(1)}, f32[16,24,768]{2,1,0:T(8,128)S(1)}) fusion(f32[768]{0:T(1024)S(1)} %get-tuple-element.49, f32[22,30,768]{2,1,0:T(8,128)S(1)} %maximum_convert_fusion, f32[768]{0:T(1024)S(1)} %get-tuple-element.50, f32[768]{0:T(1024)S(1)} %get-tuple-element.3, f32[768]{0:T(1024)S(1)} %get-tuple-element.4, ...), kind=kLoop, calls=%fused_computation.218 | loop fusion | flops 28900992 | bytes 59134464 | tf_op jit(solution)/shard_map/reduce_sum | solution.py:42
  45.9 0.3 multiply_reduce_fusion
  46.2 0.4 copy-done.7
  46.6 0.3 add_convert_fusion
  46.8 57.7 %all-gather.5.cloned.1.call-done = bf16[768,3072]{1,0:T(8,128)(2,1)} async-done(((bf16[768,768]{1,0:T(8,128)(2,1)}), bf16[768,3072]{1,0:T(8,128)(2,1)}) %all-gather.5.cloned.1.call-update) | async-done | bytes 4718608 | tf_op jit(solution)/shard_map/all_gather | solution.py:64
  104.6 89.4 %all-gather.7.cloned.1.call-done = bf16[3072,768]{1,0:T(8,128)(2,1)} async-done(((bf16[768,768]{1,0:T(8,128)(2,1)}), bf16[3072,768]{1,0:T(8,128)(2,1)}) %all-gather.7.cloned.1.call-update) | async-done | bytes 4718608 | tf_op jit(solution)/shard_map/all_gather | solution.py:69
  193.9 7.9 %fusion.34 = bf16[384,768]{1,0:T(8,128)(2,1)S(1)} fusion(bf16[3072,768]{1,0:T(8,128)(2,1)} %all-gather.7.cloned.1.call-done, bf16[384,768]{1,0:T(8,128)(2,1)S(1)} %bitcast.66, bf16[384,768]{1,0:T(8,128)(2,1)S(1)} %bitcast.70, bf16[768,3072]{1,0:T(8,128)(2,1)} %all-gather.5.cloned.1.call-done), kind=kOutput, calls=%fused_computation.37 | convolution fusion | flops 3635380224 | bytes 11206656 | tf_op jit(solution)/shard_map/dot_general | solution.py:68
  201.9 42.4 %all-gather.9.cloned.1.call-done = bf16[768,1536]{1,0:T(8,128)(2,1)} async-done(((bf16[768,384]{1,0:T(8,128)(2,1)}), bf16[768,1536]{1,0:T(8,128)(2,1)}) %all-gather.9.cloned.1.call-update) | async-done | bytes 2359312 | tf_op jit(solution)/shard_map/all_gather | solution.py:75
  244.2 2.7 convolution_convert_fusion
  247.0 0.9 fusion.111
  247.9 1.0 copy.23
  248.9 1.8 bitcast_reduce_fusion
  250.8 2.3 bitcast_reduce_fusion.1
  253.0 2.3 bitcast_reduce_fusion.2
  255.4 2.1 copy.22
  257.5 3.6 fusion.37
  261.1 3.0 fusion.11
  264.1 1.5 fusion.40
  265.6 0.5 fusion.15
  266.2 1.5 fusion.43
  267.6 39.0 %pmax.7 = f32[512,12]{0,1:T(8,128)S(1)} all-reduce(f32[512,12]{0,1:T(8,128)S(1)} %pad_maximum_fusion), channel_id=1, replica_groups=mesh['row'=8,'col'=4] {'row','col'}, use_global_device_ids=true, to_apply=%region_5.0 | all-reduce | flops 6144 | bytes 49152 | tf_op jit(solution)/shard_map/pmax | solution.py:110
  306.7 0.6 maximum_multiply_fusion.1
  307.3 2.7 maximum_multiply_fusion
  310.0 0.5 reduce-scatter.5.cloned.1.call-update
  310.6 34.6 %reduce-scatter.3.cloned.1.call-done = f32[128,768]{0,1:T(8,128)} async-done(((f32[512,768]{0,1:T(8,128)}), f32[128,768]{0,1:T(8,128)}) %reduce-scatter.3.cloned.1.call-update) | async-done | bytes 393232 | tf_op jit(solution)/shard_map/reduce_scatter | solution.py:116
  345.3 0.7 all-gather.11.cloned.1.call-update
  346.0 19.4 %reduce-scatter.5.cloned.1.call-done = f32[128,12]{0,1:T(8,128)} async-done(((f32[512,12]{0,1:T(8,128)}), f32[128,12]{0,1:T(8,128)}) %reduce-scatter.5.cloned.1.call-update) | async-done | bytes 6160 | tf_op jit(solution)/shard_map/reduce_scatter | solution.py:115
  365.4 12.2 %psum.15 = f32[128,12]{0,1:T(8,128)S(1)} all-reduce(f32[128,12]{0,1:T(8,128)} %reduce-scatter.5.cloned.1.call-done), channel_id=1, replica_groups=mesh['row'=8,'col'=4] {'row'}, use_global_device_ids=true, to_apply=%region_12.0 | all-reduce | flops 1536 | bytes 12288 | tf_op jit(solution)/shard_map/psum | solution.py:118
  377.7 43.2 %all-reduce.2.cloned.1.call-done = f32[128,768]{0,1:T(8,128)} async-done(((f32[128,768]{0,1:T(8,128)}), f32[128,768]{0,1:T(8,128)}) %all-reduce.2.cloned.1.call-update) | async-done | bytes 393232 | tf_op jit(solution)/shard_map/psum | solution.py:118
  420.9 1.1 multiply_reduce_fusion.1
  422.0 30.1 %all-gather.11.cloned.1.call-done = bf16[768,768]{0,1:T(8,128)(2,1)} async-done(((bf16[768,192]{0,1:T(8,128)(2,1)}), bf16[768,768]{0,1:T(8,128)(2,1)}) %all-gather.11.cloned.1.call-update) | async-done | bytes 1179664 | tf_op jit(solution)/shard_map/all_gather | solution.py:78
  452.1 1.9 convolution_convert_fusion.1
  454.0 17.9 %all_gather.19 = bf16[512,768]{1,0:T(8,128)(2,1)S(1)} all-gather(bf16[128,768]{1,0:T(8,128)(2,1)S(1)} %convolution_convert_fusion.1), channel_id=1, replica_groups=mesh['row'=8,'col'=4] {'col'}, dimensions={0}, use_global_device_ids=true | all-gather | bytes 983040 | tf_op jit(solution)/shard_map/all_gather | solution.py:122
  471.9 0.9 copy.35
  (41 shorter events, 0.6 us)
Async XLA Ops:
  7.2 1.6 copy-start.1
  7.2 97.4 %all-gather.5.cloned.1.call-start = ((), (), s32[]{:S(2)}) async-start(), calls=%async_computation.2 | async-start | bytes 5898240 | tf_op jit(solution)/shard_map/all_gather | solution.py:64
  7.9 4.6 copy-start.6
  7.9 4.8 %copy-start.2 = (bf16[512,768]{1,0:T(8,128)(2,1)S(1)}, bf16[512,768]{1,0:T(8,128)(2,1)}, u32[]{:S(2)}) copy-start(bf16[512,768]{1,0:T(8,128)(2,1)} %param.17) | copy-start | bytes 2359300
  7.9 186.0 %all-gather.7.cloned.1.call-start = ((), (), s32[]{:S(2)}) async-start(), calls=%async_computation.3 | async-start | bytes 5898240 | tf_op jit(solution)/shard_map/all_gather | solution.py:69
  8.7 235.6 %all-gather.9.cloned.1.call-start = ((), (), s32[]{:S(2)}) async-start(), calls=%async_computation.4 | async-start | bytes 2949120 | tf_op jit(solution)/shard_map/all_gather | solution.py:75
  8.8 5.3 %collective-permute-start = (bf16[3,24,768]{2,1,0:T(8,128)(2,1)S(1)}, bf16[3,24,768]{2,1,0:T(8,128)(2,1)S(1)}, u32[]{:S(2)}, u32[]{:S(2)}) collective-permute-start(bf16[3,24,768]{2,1,0:T(8,128)(2,1)S(1)} %get-tuple-element.62), channel_id=1, source_target_pairs={{0,4},{4,8},{8,12},{12,16},{16,20},{20,24},{24,28},{1,5},{5,9},{9,... | collective-permute-start | bytes 331784 | tf_op jit(solution)/shard_map/ppermute | solution.py:20
  11.2 5.3 %collective-permute-start.1 = (bf16[3,24,768]{2,1,0:T(8,128)(2,1)S(1)}, bf16[3,24,768]{2,1,0:T(8,128)(2,1)S(1)}, u32[]{:S(2)}, u32[]{:S(2)}) collective-permute-start(bf16[3,24,768]{2,1,0:T(8,128)(2,1)S(1)} %get-tuple-element.61), channel_id=1, source_target_pairs={{4,0},{8,4},{12,8},{16,12},{20,16},{24,20},{28,24},{5,1},{9,5},{13... | collective-permute-start | bytes 331784 | tf_op jit(solution)/shard_map/ppermute | solution.py:22
  12.5 332.7 %reduce-scatter.3.cloned.1.call-start = ((), (), s32[]{:S(2)}) async-start(), calls=%async_computation.5 | async-start | bytes 1966080 | tf_op jit(solution)/shard_map/reduce_scatter | solution.py:116
  16.6 9.2 %collective-permute-start.2 = (bf16[22,3,768]{2,1,0:T(4,128)(2,1)S(1)}, bf16[22,3,768]{2,1,0:T(4,128)(2,1)S(1)}, u32[]{:S(2)}, u32[]{:S(2)}) collective-permute-start(bf16[22,3,768]{2,1,0:T(4,128)(2,1)S(1)} %get-tuple-element.59), channel_id=1, source_target_pairs={{0,1},{1,2},{2,3},{4,5},{5,6},{6,7},{8,9},{9,10},{10,11},{12,13},{... | collective-permute-start | bytes 304136 | tf_op jit(solution)/shard_map/ppermute | solution.py:20
  20.1 13.1 %collective-permute-start.3 = (bf16[22,3,768]{2,1,0:T(4,128)(2,1)S(1)}, bf16[22,3,768]{2,1,0:T(4,128)(2,1)S(1)}, u32[]{:S(2)}, u32[]{:S(2)}) collective-permute-start(bf16[22,3,768]{2,1,0:T(4,128)(2,1)S(1)} %get-tuple-element.60), channel_id=1, source_target_pairs={{1,0},{2,1},{3,2},{5,4},{6,5},{7,6},{9,8},{10,9},{11,10},{13,12},{... | collective-permute-start | bytes 304136 | tf_op jit(solution)/shard_map/ppermute | solution.py:22
  45.9 0.7 copy-start.7
  45.9 0.7 copy-start.8
  201.9 45.1 %copy-start.10 = (bf16[384,768]{1,0:T(8,128)(2,1)}, bf16[384,768]{1,0:T(8,128)(2,1)S(1)}, u32[]{:S(2)}) copy-start(bf16[384,768]{1,0:T(8,128)(2,1)S(1)} %fusion.34) | copy-start | bytes 1769476
  248.9 1.8 copy-start.3
  248.9 1.8 copy-start.5
  257.5 3.6 copy-start
  261.1 3.0 copy-start.4
  310.0 142.2 %copy-start.9 = (f32[768]{0:T(1024)S(1)}, f32[768]{0:T(1024)}, u32[]{:S(2)}) copy-start(f32[768]{0:T(1024)} %param.18) | copy-start | bytes 9220
  310.0 55.4 %reduce-scatter.5.cloned.1.call-start = ((), (), s32[]{:S(2)}) async-start(), calls=%async_computation.7 | async-start | bytes 40960 | tf_op jit(solution)/shard_map/reduce_scatter | solution.py:115
  310.6 110.3 %all-reduce.2.cloned.1.call-start = ((), (), s32[]{:S(2)}) async-start(), calls=%async_computation.6 | async-start | bytes 786432 | tf_op jit(solution)/shard_map/psum | solution.py:118
  345.2 106.9 %all-gather.11.cloned.1.call-start = ((), (), s32[]{:S(2)}) async-start(), calls=%async_computation.8 | async-start | bytes 1474560 | tf_op jit(solution)/shard_map/all_gather | solution.py:78
Sparse Core Ops, SparseCore 0:
  9.6 94.9 all-gather.4
  106.1 87.7 all-gather.6
  195.6 48.6 all-gather.8
  310.1 35.0 reduce-scatter.2
  347.3 18.0 reduce-scatter.4
  368.4 52.5 all-reduce.1
  422.5 29.6 all-gather.10
where the time goes:
time: 480 us
  waiting for transfers between devices  334 us (70%)
  blocking collectives  69.1 us (14%)
  matrix products  25.5 us (5%)
  other arithmetic  21.2 us (4%)
  between operations  14.4 us (3%)
  starting transfers between devices  8.75 us (2%)
  local copies, waits for them, and re-layouts  7.14 us (1%)
    all_gather x1, waiting for transfers between devices, body(): lax.all_gather(w_out, 'col', axis=0, tiled=True)  89.4 us
    all_gather x1, waiting for transfers between devices, body(): lax.all_gather(w_in, 'col', axis=1, tiled=True)  57.7 us
    psum x1, waiting for transfers between devices, body(): den_share, num_share = lax.psum((den_part, num_part), 'row')  43.2 us
    all_gather x1, waiting for transfers between devices, body(): lax.all_gather(w_kv, 'col', axis=1, tiled=True)  42.4 us
    pmax x1, blocking collectives, body(): peak = lax.pmax(maxima, ('row', 'col'))  39 us
    reduce_scatter x1, waiting for transfers between devices, body(): lax.psum_scatter(num_terms, 'col', scatter_dimension=0, tiled=True)  34.6 us
    all_gather x1, waiting for transfers between devices, body(): w_full = lax.all_gather(w_o, 'col', axis=1, tiled=True)  30.1 us
    reduce_scatter x1, waiting for transfers between devices, body(): lax.psum_scatter(den_terms, 'col', scatter_dimension=0, tiled=True)  19.4 us
  transfers between devices with their start and end apart: 11, of which 10 were waited for; matrix products, arithmetic and copies ran while one was open for 5% of the time, Pallas kernels for 0%

commit v1 on v0

--- a/solution.py
+++ b/solution.py
@@ -1,12 +1,615 @@
+import functools
 import math
 
 import jax
 import jax.numpy as jnp
 from jax import lax
+from jax.experimental import pallas as pl
+from jax.experimental.pallas import tpu as pltpu
 from jax.sharding import PartitionSpec as P
 
 HEADS = 12
 HEAD = 64
+HALO = 3
+EDGE = 8
+LANES = 128
+MESH = pl.DeviceIdType.MESH
+VMEM_BYTES = 60 * 1024 * 1024
+
+
+def log2(count):
+    return count.bit_length() - 1
+
+
+def barrier_with(peers):
+    barrier = pltpu.get_barrier_semaphore()
+    total = 0
+    for cond, device in peers:
+        if cond is None:
+            pl.semaphore_signal(barrier, inc=1, device_id=device, device_id_type=MESH)
+            total = total + 1
+        else:
+
+            @pl.when(cond)
+            def _():
+                pl.semaphore_signal(barrier, inc=1, device_id=device, device_id_type=MESH)
+
+            total = total + jnp.where(cond, 1, 0)
+    pl.semaphore_wait(barrier, total)
+
+
+def block_kernel(
+    rows,
+    cols,
+    tokens,
+    left_edge,
+    right_edge,
+    dw,
+    gain,
+    shift,
+    w_in,
+    w_out,
+    w_kv,
+    w_o,
+    queries,
+    tok_out,
+    num_out,
+    stat_out,
+    wo_out,
+    g_in,
+    g_out,
+    g_kv,
+    pad,
+    mixed,
+    normed,
+    hidden,
+    acc,
+    tok_bf,
+    kv,
+    h_rows,
+    h_cols,
+    h_corners,
+    halo_send,
+    halo_recv,
+    send_sem,
+    recv_sem,
+    local_sem,
+):
+    bits = log2(rows)
+    row, col = lax.axis_index("row"), lax.axis_index("col")
+    height, width, depth = tokens.shape
+    count = height * width
+    coords = [(row // (1 << (bits - 1 - i))) % 2 for i in range(bits)]
+
+    def partner(dim):
+        step = 1 << (bits - 1 - dim)
+        return row + step * (1 - 2 * coords[dim])
+
+    halo = []
+    for dr in (-1, 0, 1):
+        for dc in (-1, 0, 1):
+            if dr == 0 and dc == 0:
+                continue
+            cond = None
+            for d, pos, n in ((dr, row, rows), (dc, col, cols)):
+                if d:
+                    one = (pos + d >= 0) & (pos + d < n)
+                    cond = one if cond is None else cond & one
+            halo.append((dr, dc, cond))
+
+    peers = [(cond, (row + dr, col + dc)) for dr, dc, cond in halo]
+    peers += [(None, (row, (col + j) % cols)) for j in range(1, cols)]
+    peers += [(None, (partner(i), col)) for i in range(bits)]
+    barrier_with(peers)
+
+    def halo_slot(dr, dc):
+        if dc == 0:
+            return h_rows.at[0 if dr < 0 else 1]
+        if dr == 0:
+            return h_cols.at[0 if dc < 0 else 1]
+        return h_corners.at[(0 if dr < 0 else 2) + (0 if dc < 0 else 1)]
+
+    def halo_copy(i, dr, dc):
+        edge = tokens if dc == 0 else (left_edge if dc < 0 else right_edge)
+        if dr == 0:
+            src = edge
+        elif dr < 0:
+            src = edge.at[pl.ds(0, HALO)]
+        else:
+            src = edge.at[pl.ds(height - HALO, HALO)]
+        return pltpu.make_async_remote_copy(
+            src_ref=src,
+            dst_ref=halo_slot(-dr, -dc),
+            send_sem=halo_send.at[i],
+            recv_sem=halo_recv.at[len(halo) - 1 - i],
+            device_id=(row + dr, col + dc),
+            device_id_type=MESH,
+        )
+
+    for i, (dr, dc, cond) in enumerate(halo):
+
+        @pl.when(cond)
+        def _():
+            halo_copy(i, dr, dc).start()
+
+    shards = (w_in, w_out, w_kv, w_o)
+    fulls = (g_in, g_out, g_kv, wo_out)
+    units = [(w, j) for w in range(4) for j in range(1, cols)]
+    own = tuple(coords)
+
+    def unit_copy(u, phase):
+        w, j = units[u]
+        if phase == 0:
+            target = (row, (col + cols - j) % cols)
+            src = shards[w].at[own]
+            dst = fulls[w].at[(col,) + own]
+        else:
+            order = list(range(bits - 1))
+            if u % 2:
+                order = order[::-1]
+            order = order + [bits - 1]
+            done = order[: phase - 1]
+            block = (col + j) % cols
+            idx = (block,) + tuple(slice(None) if i in done else own[i] for i in range(bits))
+            src = fulls[w].at[idx]
+            dst = fulls[w].at[idx]
+            target = (partner(order[phase - 1]), col)
+        slot = u * (bits + 1) + phase
+        return pltpu.make_async_remote_copy(
+            src_ref=src,
+            dst_ref=dst,
+            send_sem=send_sem.at[slot],
+            recv_sem=recv_sem.at[slot],
+            device_id=target,
+            device_id_type=MESH,
+        )
+
+    for u in range(len(units)):
+        unit_copy(u, 0).start()
+    local = []
+    for w in range(4):
+        copy = pltpu.make_async_copy(shards[w], fulls[w].at[col], local_sem.at[w])
+        copy.start()
+        local.append(copy)
+
+    state = {"tick": 0}
+    ticks = len(units) + bits
+
+    def tick():
+        t = state["tick"]
+        if t >= ticks:
+            return
+        state["tick"] = t + 1
+        for phase in range(bits, -1, -1):
+            u = t - phase
+            if 0 <= u < len(units):
+                unit_copy(u, phase).wait_recv()
+                if phase < bits:
+                    unit_copy(u, phase + 1).start()
+
+    def finish_unit(u):
+        while state["tick"] <= u + bits:
+            tick()
+
+    pad[pl.ds(HALO, height), pl.ds(EDGE, width), :] = tokens[...].astype(jnp.float32)
+    spans = {-1: (0, HALO), 0: (HALO, height), 1: (HALO + height, HALO)}
+    lanes_of = {-1: (0, EDGE), 0: (EDGE, width), 1: (EDGE + width, EDGE)}
+    for i, (dr, dc, cond) in enumerate(halo):
+        r0, rn = spans[dr]
+        c0, cn = lanes_of[dc]
+
+        @pl.when(cond)
+        def _():
+            halo_copy(len(halo) - 1 - i, -dr, -dc).wait_recv()
+            pad[pl.ds(r0, rn), pl.ds(c0, cn), :] = halo_slot(dr, dc)[...].astype(jnp.float32)
+
+        @pl.when(jnp.logical_not(cond))
+        def _():
+            pad[pl.ds(r0, rn), pl.ds(c0, cn), :] = jnp.zeros((rn, cn, depth), jnp.float32)
+
+    taps = 2 * HALO + 1
+    chunks = depth // LANES
+
+    def conv_rows(first, n_rows):
+        def one(step, carry):
+            i = first + step // chunks
+            q = pl.multiple_of((step % chunks) * LANES, LANES)
+            sums = [None] * taps
+            for a in range(taps):
+                line = pad[i + a, :, pl.ds(q, LANES)]
+                for b in range(taps):
+                    lo = 0 if b < HALO else EDGE
+                    hi = EDGE + width + (EDGE if b > HALO else 0)
+                    term = line[lo:hi] * dw[a, pl.ds(b, 1), pl.ds(q, LANES)]
+                    sums[b] = term if sums[b] is None else sums[b] + term
+            total = sums[HALO]
+            for b in range(taps):
+                if b == HALO:
+                    continue
+                size = width + EDGE
+                offset = EDGE - HALO + b - (0 if b < HALO else EDGE)
+                total = total + pltpu.roll(sums[b], (size - offset) % size, 0)[:width]
+            mixed[i, :, pl.ds(q, LANES)] = total
+            return carry
+
+        lax.fori_loop(0, n_rows * chunks, one, 0)
+
+    group = 2
+    span = group * width
+
+    def norm_rows(g, carry):
+        value = mixed[pl.ds(g * group, group), :, :].reshape(span, depth)
+        center = value - jnp.mean(value, axis=-1, keepdims=True)
+        spread = jnp.mean(center * center, axis=-1, keepdims=True)
+        out = center * lax.rsqrt(spread + 1e-06) * gain[...] + shift[...]
+        normed[pl.ds(pl.multiple_of(g * span, 16), span), :] = out.astype(jnp.bfloat16)
+        return carry
+
+    quarter = height // 4
+    for part in range(4):
+        conv_rows(part * quarter, quarter)
+        tick()
+    lax.fori_loop(0, height // group, norm_rows, 0)
+    for copy in local:
+        copy.wait()
+
+    def wide(ref, block, lo, size):
+        value = ref[(block,) + (slice(None),) * (bits + 1) + (pl.ds(lo, size),)]
+        return value.reshape(-1, size)
+
+    f_width = w_in.shape[-1]
+    tile = 256 if f_width % 256 == 0 else LANES
+
+    def expand(block):
+        def one(n, carry):
+            lo = pl.multiple_of(n * tile, tile)
+            u = jnp.dot(normed[...], wide(g_in, block, lo, tile), preferred_element_type=jnp.float32)
+            hidden[block, :, pl.ds(lo, tile)] = jax.nn.gelu(u).astype(jnp.bfloat16)
+            return carry
+
+        lax.fori_loop(0, f_width // tile, one, 0)
+
+    def contract(block, fresh):
+        def one(n, carry):
+            lo = pl.multiple_of(n * 256, 256)
+            part = jnp.dot(
+                hidden[block], wide(g_out, block, lo, 256), preferred_element_type=jnp.float32
+            )
+            if fresh:
+                acc[:, pl.ds(lo, 256)] = part
+            else:
+                acc[:, pl.ds(lo, 256)] += part
+            return carry
+
+        lax.fori_loop(0, depth // 256, one, 0)
+
+    expand(col)
+    tick()
+    contract(col, True)
+    for j in range(1, cols):
+        finish_unit(j - 1)
+        expand((col + j) % cols)
+    for j in range(1, cols):
+        finish_unit(cols - 1 + j - 1)
+        contract((col + j) % cols, False)
+
+    def close_rows(g, carry):
+        base = pad[pl.ds(HALO + g * group, group), pl.ds(EDGE, width), :].reshape(span, depth)
+        at = pl.ds(pl.multiple_of(g * span, 16), span)
+        total = base + acc[at, :]
+        tok_out[pl.ds(g * group, group), :, :] = total.reshape(group, width, depth).astype(jnp.bfloat16)
+        tok_bf[at, :] = total.astype(jnp.bfloat16)
+        return carry
+
+    lax.fori_loop(0, height // group, close_rows, 0)
+
+    kv_width = w_kv.shape[-1]
+
+    def project(block):
+        def one(n, carry):
+            lo = pl.multiple_of(n * LANES, LANES)
+            out = jnp.dot(tok_bf[...], wide(g_kv, block, lo, LANES), preferred_element_type=jnp.float32)
+            kv[block, :, pl.ds(lo, LANES)] = out.astype(jnp.bfloat16)
+            return carry
+
+        lax.fori_loop(0, kv_width // LANES, one, 0)
+
+    project(col)
+    for j in range(1, cols):
+        finish_unit(2 * (cols - 1) + j - 1)
+        project((col + j) % cols)
+
+    latents = queries.shape[0]
+    scale = 1.0 / math.sqrt(HEAD)
+    stat_out[...] = jnp.zeros((latents, LANES), jnp.float32)
+    side = lax.broadcasted_iota(jnp.int32, (1, LANES), 1)
+
+    def attend(pair, carry):
+        at = pl.multiple_of(pair * LANES, LANES)
+        k_at, v_at = at, depth + at
+        keys = kv[k_at // kv_width, :, pl.ds(pl.multiple_of(k_at % kv_width, LANES), LANES)]
+        vals = kv[v_at // kv_width, :, pl.ds(pl.multiple_of(v_at % kv_width, LANES), LANES)]
+        q = queries[:, pl.ds(at, LANES)]
+        stat = stat_out[...]
+        outs = []
+        for s in range(2):
+            keep = (side // HEAD) == s
+            q_one = jnp.where(keep, q, jnp.zeros_like(q))
+            scores = lax.dot_general(
+                q_one, keys, (((1,), (1,)), ((), ())), preferred_element_type=jnp.float32
+            )
+            top = jnp.max(scores, axis=-1, keepdims=True)
+            weights = jnp.exp((scores - top) * scale)
+            den = jnp.sum(weights, axis=-1, keepdims=True)
+            outs.append(
+                jnp.dot(weights.astype(jnp.bfloat16), vals, preferred_element_type=jnp.float32)
+            )
+            lane = pair * 2 + s
+            stat = jnp.where(side == lane, top * scale, stat)
+            stat = jnp.where(side == lane + HEAD, den, stat)
+        stat_out[...] = stat
+        num_out[:, pl.ds(at, LANES)] = jnp.where(side < HEAD, outs[0], outs[1]).astype(jnp.bfloat16)
+        return carry
+
+    lax.fori_loop(0, depth // LANES, attend, 0)
+
+    finish_unit(len(units) - 1)
+    for i, (dr, dc, cond) in enumerate(halo):
+
+        @pl.when(cond)
+        def _():
+            halo_copy(i, dr, dc).wait_send()
+
+    for u in range(len(units)):
+        for phase in range(bits + 1):
+            unit_copy(u, phase).wait_send()
+
+
+def per_head(factors, n):
+    side = lax.broadcasted_iota(jnp.int32, (1, LANES), 1)
+    parts = []
+    for pair in range(HEADS // 2):
+        lo = jnp.broadcast_to(factors[:, 2 * pair : 2 * pair + 1], (n, LANES))
+        hi = jnp.broadcast_to(factors[:, 2 * pair + 1 : 2 * pair + 2], (n, LANES))
+        parts.append(jnp.where(side < HEAD, lo, hi))
+    return jnp.concatenate(parts, axis=-1)
+
+
+def merge(stats, nums):
+    n = stats[0].shape[0]
+    side = lax.broadcasted_iota(jnp.int32, (1, LANES), 1)
+    peak = functools.reduce(jnp.maximum, stats)
+    den, num = None, None
+    for stat, part in zip(stats, nums):
+        factor = jnp.exp(stat - peak)
+        d = pltpu.roll(stat, HEAD, 1) * factor
+        t = part.astype(jnp.float32) * per_head(factor, n)
+        den = d if den is None else den + d
+        num = t if num is None else num + t
+    return jnp.where(side < HEAD, peak, pltpu.roll(den, HEAD, 1)), num
+
+
+def latent_kernel(
+    rows, cols, num_in, stat_in, latent_gain, out, num, stat, got_num, got_stat, send_sem, recv_sem
+):
+    bits = log2(rows)
+    row, col = lax.axis_index("row"), lax.axis_index("col")
+    latents = num_in.shape[0]
+
+    def bit(i):
+        return (row // (1 << i)) % 2
+
+    def partner(i):
+        return row + (1 << i) * (1 - 2 * bit(i))
+
+    peers = [(None, (row, (col + j) % cols)) for j in range(1, cols)]
+    peers += [(None, (partner(i), col)) for i in range(bits)]
+    barrier_with(peers)
+
+    def copy(src, dst, slot, device):
+        return pltpu.make_async_remote_copy(
+            src_ref=src,
+            dst_ref=dst,
+            send_sem=send_sem.at[slot],
+            recv_sem=recv_sem.at[slot],
+            device_id=device,
+            device_id_type=MESH,
+        )
+
+    slot = 0
+    sent = []
+    base = 0
+    size = latents
+    offset = 0
+    bases = []
+    for i in range(bits):
+        half = size // 2
+        mine = base + bit(i) * half
+        theirs = base + (1 - bit(i)) * half
+        src_num, src_stat = (num_in, stat_in) if i == 0 else (num, stat)
+        give = pl.ds(pl.multiple_of(theirs, 16), half)
+        land = pl.ds(offset, half)
+        pair = [
+            copy(src_stat.at[give], got_stat.at[land], slot, (partner(i), col)),
+            copy(src_num.at[give], got_num.at[land], slot + 1, (partner(i), col)),
+        ]
+        slot += 2
+        for c in pair:
+            c.start()
+        for c in pair:
+            c.wait_recv()
+        sent += pair
+        step = min(half, 32)
+
+        def fold(k, carry):
+            at = pl.ds(pl.multiple_of(mine + k * step, 16), step)
+            came = pl.ds(pl.multiple_of(offset + k * step, 16), step)
+            new_stat, new_num = merge(
+                [src_stat[at, :], got_stat[came, :]], [src_num[at, :], got_num[came, :]]
+            )
+            stat[at, :] = new_stat
+            num[at, :] = new_num.astype(jnp.bfloat16)
+            return carry
+
+        lax.fori_loop(0, half // step, fold, 0)
+        bases.append((base, size))
+        base, size, offset = mine, half, offset + half
+
+    share = size // cols
+    arrived = []
+    for j in range(1, cols):
+        other = (col + cols - j) % cols
+        give = pl.ds(pl.multiple_of(base + other * share, 16), share)
+        land = pl.ds(offset + (j - 1) * share, share)
+        pair = [
+            copy(stat.at[give], got_stat.at[land], slot, (row, other)),
+            copy(num.at[give], got_num.at[land], slot + 1, (row, other)),
+        ]
+        slot += 2
+        for c in pair:
+            c.start()
+        sent += pair
+        arrived.append((pair, land))
+    for pair, _ in arrived:
+        for c in pair:
+            c.wait_recv()
+    own = pl.ds(pl.multiple_of(base + col * share, 16), share)
+    final_stat, final_num = merge(
+        [stat[own, :]] + [got_stat[land, :] for _, land in arrived],
+        [num[own, :]] + [got_num[land, :] for _, land in arrived],
+    )
+    attended = final_num / per_head(pltpu.roll(final_stat, HEAD, 1), share)
+    squares = jnp.mean(attended * attended, axis=-1, keepdims=True)
+    scaled = attended * lax.rsqrt(squares + 1e-06) * latent_gain[...]
+    out[own, :] = scaled.astype(jnp.bfloat16)
+
+    gather = []
+    for j in range(1, cols):
+        c = copy(out.at[own], out.at[own], slot, (row, (col + cols - j) % cols))
+        slot += 1
+        c.start()
+        gather.append(c)
+    for c in gather:
+        c.wait_recv()
+    sent += gather
+    for i in reversed(range(bits)):
+        held = pl.ds(pl.multiple_of(base, 16), size)
+        c = copy(out.at[held], out.at[held], slot, (partner(i), col))
+        slot += 1
+        c.start()
+        c.wait_recv()
+        sent.append(c)
+        base, size = bases[i]
+    for c in sent:
+        c.wait_send()
+
+
+def vmem(n):
+    return [pl.BlockSpec(memory_space=pltpu.VMEM)] * n
+
+
+def fits(mesh_rows, mesh_cols, tokens, w_in, w_kv, queries):
+    height, width, depth = tokens.shape
+    return (
+        mesh_rows >= 2
+        and mesh_cols >= 2
+        and mesh_rows & (mesh_rows - 1) == 0
+        and depth % (16 * mesh_rows) == 0
+        and w_in.shape[1] % LANES == 0
+        and w_kv.shape[1] % LANES == 0
+        and queries.shape[0] % (16 * mesh_rows * mesh_cols) == 0
+        and depth % 256 == 0
+        and height % 4 == 0
+        and width % 8 == 0
+        and 2 * width % 16 == 0
+    )
+
+
+def kernel_body(tokens, dw_kernel, norm_gain, norm_shift, w_in, w_out, w_kv, queries, latent_gain, w_o):
+    rows, cols = lax.axis_size("row"), lax.axis_size("col")
+    height, width, depth = tokens.shape
+    if not fits(rows, cols, tokens, w_in, w_kv, queries):
+        return body(
+            tokens, dw_kernel, norm_gain, norm_shift, w_in, w_out, w_kv, queries, latent_gain, w_o
+        )
+    bits = log2(rows)
+    count = height * width
+    latents = queries.shape[0]
+    f_width = w_in.shape[1]
+    grid = (2,) * bits
+    bf16, f32 = jnp.bfloat16, jnp.float32
+
+    def cut(w):
+        return w.reshape(grid + (w.shape[0] // rows, w.shape[1]))
+
+    shards = [cut(w) for w in (w_in, w_out, w_kv, w_o)]
+    units = 4 * (cols - 1)
+    token_map, num, stat, wo_full = pl.pallas_call(
+        functools.partial(block_kernel, rows, cols),
+        out_shape=(
+            jax.ShapeDtypeStruct(tokens.shape, bf16),
+            jax.ShapeDtypeStruct((latents, depth), bf16),
+            jax.ShapeDtypeStruct((latents, LANES), f32),
+            jax.ShapeDtypeStruct((cols,) + shards[3].shape, bf16),
+        ),
+        in_specs=vmem(11),
+        out_specs=tuple(vmem(4)),
+        scratch_shapes=[
+            pltpu.VMEM((cols,) + shards[0].shape, bf16),
+            pltpu.VMEM((cols,) + shards[1].shape, bf16),
+            pltpu.VMEM((cols,) + shards[2].shape, bf16),
+            pltpu.VMEM((height + 2 * HALO, width + 2 * EDGE, depth), f32),
+            pltpu.VMEM((height, width, depth), f32),
+            pltpu.VMEM((count, depth), bf16),
+            pltpu.VMEM((cols, count, f_width), bf16),
+            pltpu.VMEM((count, depth), f32),
+            pltpu.VMEM((count, depth), bf16),
+            pltpu.VMEM((cols, count, w_kv.shape[1]), bf16),
+            pltpu.VMEM((2, HALO, width, depth), bf16),
+            pltpu.VMEM((2, height, EDGE, depth), bf16),
+            pltpu.VMEM((4, HALO, EDGE, depth), bf16),
+            pltpu.SemaphoreType.DMA((8,)),
+            pltpu.SemaphoreType.DMA((8,)),
+            pltpu.SemaphoreType.DMA((units * (bits + 1),)),
+            pltpu.SemaphoreType.DMA((units * (bits + 1),)),
+            pltpu.SemaphoreType.DMA((4,)),
+        ],
+        compiler_params=pltpu.CompilerParams(
+            collective_id=0, has_side_effects=True, vmem_limit_bytes=VMEM_BYTES
+        ),
+        name="block",
+    )(
+        tokens,
+        tokens[:, :EDGE],
+        tokens[:, width - EDGE :],
+        dw_kernel,
+        norm_gain.reshape(1, depth),
+        norm_shift.reshape(1, depth),
+        *shards,
+        queries,
+    )
+    slots = 2 * bits + 3 * (cols - 1) + bits
+    scaled = pl.pallas_call(
+        functools.partial(latent_kernel, rows, cols),
+        out_shape=jax.ShapeDtypeStruct((latents, depth), bf16),
+        in_specs=vmem(3),
+        out_specs=vmem(1)[0],
+        scratch_shapes=[
+            pltpu.VMEM((latents, depth), bf16),
+            pltpu.VMEM((latents, LANES), f32),
+            pltpu.VMEM((latents, depth), bf16),
+            pltpu.VMEM((latents, LANES), f32),
+            pltpu.SemaphoreType.DMA((slots,)),
+            pltpu.SemaphoreType.DMA((slots,)),
+        ],
+        compiler_params=pltpu.CompilerParams(
+            collective_id=1, has_side_effects=True, vmem_limit_bytes=VMEM_BYTES
+        ),
+        name="latents",
+    )(num, stat, latent_gain.reshape(1, depth))
+    w_full = wo_full.reshape(cols, depth, -1).transpose(1, 0, 2).reshape(depth, -1)
+    latents_out = jnp.dot(scaled, w_full, preferred_element_type=f32).astype(bf16)
+    return (token_map, latents_out)
 
 
 def with_halo(cells, sides, width):
@@ -137,4 +740,4 @@
         P(None, "col"),
     )
     out_specs = (P("row", "col", None), P())
-    return jax.shard_map(body, mesh=mesh, in_specs=in_specs, out_specs=out_specs, check_vma=False)
+    return jax.shard_map(kernel_body, mesh=mesh, in_specs=in_specs, out_specs=out_specs, check_vma=False)

time: 480 us -> 174 us (0.36)
  waiting for transfers between devices: 334 us -> 0 us
  Pallas kernels: 0 us -> 162 us
  blocking collectives: 69.1 us -> 0 us
  matrix products: 25.5 us -> 1.69 us
  other arithmetic: 21.2 us -> 0 us
  between operations: 14.4 us -> 0.68 us
  starting transfers between devices: 8.75 us -> 0 us
    all_gather x4 -> x0, waiting for transfers between devices: 220 us -> none  [the longest x1 89.4 us: body(): lax.all_gather(w_out, 'col', axis=0, tiled=True)]
    pallas_call x0 -> x2, Pallas kernels: none -> 162 us  [the longest x1 121 us: kernel_body(): pl.pallas_call(functools.partial(block_kernel, rows, cols), out_shape=(ja...]
    reduce_scatter x2 -> x0, waiting for transfers between devices: 54 us -> none  [the longest x1 34.6 us: body(): lax.psum_scatter(num_terms, 'col', scatter_dimension=0, tiled=True)]
    psum x1 -> x0, waiting for transfers between devices: 43.2 us -> none  [body(): den_share, num_share = lax.psum((den_part, num_part), 'row')]
    pmax x1 -> x0, blocking collectives: 39 us -> none  [body(): peak = lax.pmax(maxima, ('row', 'col'))]
    dot_general x9 -> x1, matrix products: 25.5 us -> 1.69 us  [kernel_body(): jnp.dot(scaled, w_full, preferred_element_type=f32).astype(bf16)]
    all_gather x1 -> x0, blocking collectives: 17.9 us -> none  [body(): latents = lax.all_gather(own_rows, 'col', axis=0, tiled=True)]
    reduce_sum x5 -> x0, other arithmetic: 17.2 us -> none  [the longest x1 12.3 us: layer_norm(): center = mixed - jnp.mean(mixed, axis=-1, keepdims=True)]
  transfers between devices with their start and end apart: 11 -> 0, of which waited for: 10 -> 0; matrix products, arithmetic and copies ran while one was open for 5% -> 0% of each run, Pallas kernels for 0% -> 0%
where the time goes in v1:
time: 174 us
  Pallas kernels  162 us (93%)
  local copies, waits for them, and re-layouts  9.43 us (5%)
    pallas_call x1, Pallas kernels, kernel_body(): pl.pallas_call(functools.partial(block_kernel, rows, cols), out_shape=(ja...  121 us
    pallas_call x1, Pallas kernels, kernel_body(): pl.pallas_call(functools.partial(latent_kernel, rows, cols), out_shape=ja...  41.8 us

profile of v1, /device:TPU:0, one launch (start us, length us, event | category | flops | bytes accessed | tf_op | source)
XLA Modules:
  0.0 174.1 jit_solution(16506188348122004301)
XLA Ops:
  0.6 1.3 reshape.31.gain
  1.9 1.3 reshape.32.shift
  3.2 1.3 reshape.37.latent_gain
  4.4 1.9 %copy.13 = bf16[768,192]{1,0:T(8,128)(2,1)} copy(bf16[768,192]{0,1:T(8,128)(2,1)} %param.19) | data formatting | bytes 589824 | tf_op args[9]
  6.3 1.8 %fusion = (bf16[16,8,768]{2,1,0:T(8,128)(2,1)}, bf16[16,8,768]{2,1,0:T(8,128)(2,1)}) fusion(bf16[16,24,768]{2,1,0:T(8,128)(2,1)} %tokens.1), kind=kLoop, calls=%fused_computation.1 | loop fusion | bytes 786432 | tf_op jit(solution)/shard_map/slice | solution.py:584
  8.1 120.6 %block.1 = (bf16[16,24,768]{2,1,0:T(8,128)(2,1)}, bf16[512,768]{1,0:T(8,128)(2,1)}, f32[512,128]{1,0:T(8,128)}, bf16[4,2,2,2,96,192]{5,4,3,2,1,0:T(8,128)(2,1)}) custom-call(bf16[16,24,768]{2,1,0:T(8,128)(2,1)} %tokens.1, bf16[16,8,768]{2,1,0:T(8,128)(2,1)} %get-tuple-element.11.left_edge, bf16[16,8,768]{2,1,0:T(8,128)(2,1)} %get-tuple-element.10.right_edge, ...), custom_call_target="tpu_custom_call" | custom-call | tf_op jit(solution)/shard_map/block/pallas_call | solution.py:547
  128.7 0.0 copy-start
  128.7 41.8 %latents.1 = bf16[512,768]{1,0:T(8,128)(2,1)} custom-call(bf16[512,768]{1,0:T(8,128)(2,1)} %get-tuple-element.7.num_in, f32[512,128]{1,0:T(8,128)} %get-tuple-element.8.stat_in, f32[1,768]{1,0:T(1,128)} %reshape.37.latent_gain), custom_call_target="tpu_custom_call" | custom-call | tf_op jit(solution)/shard_map/latents/pallas_call | solution.py:592
  170.5 0.0 copy-done
  170.5 0.0 copy-start.1
  170.5 0.7 copy.14
  171.2 0.4 copy-done.1
  171.6 0.0 copy-start.2
  171.6 1.7 convolution_convert_fusion
  173.3 0.0 copy-done.2
  173.3 0.8 copy.16
Async XLA Ops:
  128.7 41.8 %copy-start = (bf16[4,2,2,2,96,192]{5,4,3,2,1,0:T(8,128)(2,1)S(1)}, bf16[4,2,2,2,96,192]{5,4,3,2,1,0:T(8,128)(2,1)}, u32[]{:S(2)}) copy-start(bf16[4,2,2,2,96,192]{5,4,3,2,1,0:T(8,128)(2,1)} %get-tuple-element.9) | copy-start | bytes 3538948
  170.5 1.1 copy-start.1
  171.6 1.7 copy-start.2

commit v2 on v1

--- a/solution.py
+++ b/solution.py
@@ -42,8 +42,6 @@
     rows,
     cols,
     tokens,
-    left_edge,
-    right_edge,
     dw,
     gain,
     shift,
@@ -110,13 +108,9 @@
         return h_corners.at[(0 if dr < 0 else 2) + (0 if dc < 0 else 1)]
 
     def halo_copy(i, dr, dc):
-        edge = tokens if dc == 0 else (left_edge if dc < 0 else right_edge)
-        if dr == 0:
-            src = edge
-        elif dr < 0:
-            src = edge.at[pl.ds(0, HALO)]
-        else:
-            src = edge.at[pl.ds(height - HALO, HALO)]
+        r_span = {-1: pl.ds(0, HALO), 0: slice(None), 1: pl.ds(height - HALO, HALO)}[dr]
+        c_span = {-1: pl.ds(0, EDGE), 0: slice(None), 1: pl.ds(width - EDGE, EDGE)}[dc]
+        src = tokens.at[r_span, c_span]
         return pltpu.make_async_remote_copy(
             src_ref=src,
             dst_ref=halo_slot(-dr, -dc),
@@ -137,43 +131,55 @@
     units = [(w, j) for w in range(4) for j in range(1, cols)]
     own = tuple(coords)
 
-    def unit_copy(u, phase):
+    halves = [len(w.shape) - bits - 2 for w in shards]
+    ways = bits + (bits - 1) + 1
+
+    def unit_copies(u, phase):
         w, j = units[u]
+        slot = u * ways
         if phase == 0:
             target = (row, (col + cols - j) % cols)
-            src = shards[w].at[own]
-            dst = fulls[w].at[(col,) + own]
+            trips = [(shards[w].at[own], fulls[w].at[(col,) + own], target, slot)]
         else:
-            order = list(range(bits - 1))
-            if u % 2:
-                order = order[::-1]
-            order = order + [bits - 1]
-            done = order[: phase - 1]
             block = (col + j) % cols
-            idx = (block,) + tuple(slice(None) if i in done else own[i] for i in range(bits))
-            src = fulls[w].at[idx]
-            dst = fulls[w].at[idx]
-            target = (partner(order[phase - 1]), col)
-        slot = u * (bits + 1) + phase
-        return pltpu.make_async_remote_copy(
-            src_ref=src,
-            dst_ref=dst,
-            send_sem=send_sem.at[slot],
-            recv_sem=recv_sem.at[slot],
-            device_id=target,
-            device_id_type=MESH,
-        )
+            split = halves[w] and phase < bits
+            trips = []
+            for half in range(2 if split else 1):
+                order = list(range(bits - 1))
+                if (half if split else u % 2):
+                    order = order[::-1]
+                order = order + [bits - 1]
+                done = order[: phase - 1]
+                idx = (block,) + tuple(slice(None) if i in done else own[i] for i in range(bits))
+                if split:
+                    idx = idx + (half,)
+                ref = fulls[w].at[idx]
+                at = slot + ways - 1 if phase == bits else slot + 1 + 2 * (phase - 1) + half
+                trips.append((ref, ref, (partner(order[phase - 1]), col), at))
+        return [
+            pltpu.make_async_remote_copy(
+                src_ref=src,
+                dst_ref=dst,
+                send_sem=send_sem.at[at],
+                recv_sem=recv_sem.at[at],
+                device_id=target,
+                device_id_type=MESH,
+            )
+            for src, dst, target, at in trips
+        ]
 
     for u in range(len(units)):
-        unit_copy(u, 0).start()
+        for c in unit_copies(u, 0):
+            c.start()
     local = []
     for w in range(4):
         copy = pltpu.make_async_copy(shards[w], fulls[w].at[col], local_sem.at[w])
         copy.start()
         local.append(copy)
 
+    lag = 2
     state = {"tick": 0}
-    ticks = len(units) + bits
+    ticks = len(units) + lag * bits
 
     def tick():
         t = state["tick"]
@@ -181,14 +187,16 @@
             return
         state["tick"] = t + 1
         for phase in range(bits, -1, -1):
-            u = t - phase
+            u = t - lag * phase
             if 0 <= u < len(units):
-                unit_copy(u, phase).wait_recv()
+                for c in unit_copies(u, phase):
+                    c.wait_recv()
                 if phase < bits:
-                    unit_copy(u, phase + 1).start()
+                    for c in unit_copies(u, phase + 1):
+                        c.start()
 
     def finish_unit(u):
-        while state["tick"] <= u + bits:
+        while state["tick"] <= u + lag * bits:
             tick()
 
     pad[pl.ds(HALO, height), pl.ds(EDGE, width), :] = tokens[...].astype(jnp.float32)
@@ -241,7 +249,7 @@
         value = mixed[pl.ds(g * group, group), :, :].reshape(span, depth)
         center = value - jnp.mean(value, axis=-1, keepdims=True)
         spread = jnp.mean(center * center, axis=-1, keepdims=True)
-        out = center * lax.rsqrt(spread + 1e-06) * gain[...] + shift[...]
+        out = center * lax.rsqrt(spread + 1e-06) * gain[...][None, :] + shift[...][None, :]
         normed[pl.ds(pl.multiple_of(g * span, 16), span), :] = out.astype(jnp.bfloat16)
         return carry
 
@@ -254,7 +262,7 @@
         copy.wait()
 
     def wide(ref, block, lo, size):
-        value = ref[(block,) + (slice(None),) * (bits + 1) + (pl.ds(lo, size),)]
+        value = ref[(block,) + (slice(None),) * (bits + 2) + (pl.ds(lo, size),)]
         return value.reshape(-1, size)
 
     f_width = w_in.shape[-1]
@@ -362,7 +370,8 @@
 
     for u in range(len(units)):
         for phase in range(bits + 1):
-            unit_copy(u, phase).wait_send()
+            for c in unit_copies(u, phase):
+                c.wait_send()
 
 
 def per_head(factors, n):
@@ -480,7 +489,7 @@
     )
     attended = final_num / per_head(pltpu.roll(final_stat, HEAD, 1), share)
     squares = jnp.mean(attended * attended, axis=-1, keepdims=True)
-    scaled = attended * lax.rsqrt(squares + 1e-06) * latent_gain[...]
+    scaled = attended * lax.rsqrt(squares + 1e-06) * latent_gain[...][None, :]
     out[own, :] = scaled.astype(jnp.bfloat16)
 
     gather = []
@@ -514,8 +523,10 @@
         mesh_rows >= 2
         and mesh_cols >= 2
         and mesh_rows & (mesh_rows - 1) == 0
-        and depth % (16 * mesh_rows) == 0
+        and depth % (32 * mesh_rows) == 0
         and w_in.shape[1] % LANES == 0
+        and w_in.shape[1] % (32 * mesh_rows) == 0
+        and depth // mesh_cols % (8 * mesh_rows) == 0
         and w_kv.shape[1] % LANES == 0
         and queries.shape[0] % (16 * mesh_rows * mesh_cols) == 0
         and depth % 256 == 0
@@ -539,10 +550,11 @@
     grid = (2,) * bits
     bf16, f32 = jnp.bfloat16, jnp.float32
 
-    def cut(w):
-        return w.reshape(grid + (w.shape[0] // rows, w.shape[1]))
-
-    shards = [cut(w) for w in (w_in, w_out, w_kv, w_o)]
+    def cut(w, parts):
+        tail = (2, w.shape[0] // rows // 2) if parts == 2 else (w.shape[0] // rows,)
+        return w.reshape(grid + tail + (w.shape[1],))
+
+    shards = [cut(w_in, 2), cut(w_out, 2), cut(w_kv, 2), cut(w_o.T, 1)]
     units = 4 * (cols - 1)
     token_map, num, stat, wo_full = pl.pallas_call(
         functools.partial(block_kernel, rows, cols),
@@ -552,7 +564,7 @@
             jax.ShapeDtypeStruct((latents, LANES), f32),
             jax.ShapeDtypeStruct((cols,) + shards[3].shape, bf16),
         ),
-        in_specs=vmem(11),
+        in_specs=vmem(9),
         out_specs=tuple(vmem(4)),
         scratch_shapes=[
             pltpu.VMEM((cols,) + shards[0].shape, bf16),
@@ -570,8 +582,8 @@
             pltpu.VMEM((4, HALO, EDGE, depth), bf16),
             pltpu.SemaphoreType.DMA((8,)),
             pltpu.SemaphoreType.DMA((8,)),
-            pltpu.SemaphoreType.DMA((units * (bits + 1),)),
-            pltpu.SemaphoreType.DMA((units * (bits + 1),)),
+            pltpu.SemaphoreType.DMA((units * 2 * bits,)),
+            pltpu.SemaphoreType.DMA((units * 2 * bits,)),
             pltpu.SemaphoreType.DMA((4,)),
         ],
         compiler_params=pltpu.CompilerParams(
@@ -580,11 +592,9 @@
         name="block",
     )(
         tokens,
-        tokens[:, :EDGE],
-        tokens[:, width - EDGE :],
         dw_kernel,
-        norm_gain.reshape(1, depth),
-        norm_shift.reshape(1, depth),
+        norm_gain,
+        norm_shift,
         *shards,
         queries,
     )
@@ -606,9 +616,11 @@
             collective_id=1, has_side_effects=True, vmem_limit_bytes=VMEM_BYTES
         ),
         name="latents",
-    )(num, stat, latent_gain.reshape(1, depth))
-    w_full = wo_full.reshape(cols, depth, -1).transpose(1, 0, 2).reshape(depth, -1)
-    latents_out = jnp.dot(scaled, w_full, preferred_element_type=f32).astype(bf16)
+    )(num, stat, latent_gain)
+    w_turned = wo_full.reshape(-1, depth)
+    latents_out = lax.dot_general(
+        scaled, w_turned, (((1,), (1,)), ((), ())), preferred_element_type=f32
+    ).astype(bf16)
     return (token_map, latents_out)
 
 

time: 174 us -> 129 us (0.74)
  Pallas kernels: 162 us -> 125 us
  local copies, waits for them, and re-layouts: 9.43 us -> 0.82 us
    pallas_call x1, Pallas kernels: 121 us -> 83.5 us  [kernel_body(): pl.pallas_call(functools.partial(block_kernel, rows, cols), out_shape=(ja...]
    reshape x4 -> x0, local copies, waits for them, and re-layouts: 4.48 us -> none  [the longest x1 1.28 us: kernel_body(): norm_shift.reshape(1, depth)]
    unnamed x8 -> x5, local copies, waits for them, and re-layouts: 3.15 us -> 0.82 us
    slice x1 -> x0, local copies, waits for them, and re-layouts: 1.8 us -> none  [kernel_body(): tokens[:, width - EDGE:]]
where the time goes in v2:
time: 129 us
  Pallas kernels  125 us (97%)
  matrix products  2.88 us (2%)
    pallas_call x1, Pallas kernels, kernel_body(): pl.pallas_call(functools.partial(block_kernel, rows, cols), out_shape=(ja...  83.5 us
    pallas_call x1, Pallas kernels, kernel_body(): pl.pallas_call(functools.partial(latent_kernel, rows, cols), out_shape=ja...  41.4 us
    dot_general x1, matrix products, kernel_body(): lax.dot_general(scaled, w_turned, (((1,), (1,)), ((), ())), preferred_ele...  2.88 us

profile of v2, /device:TPU:0, one launch (start us, length us, event | category | flops | bytes accessed | tf_op | source)
XLA Modules:
  0.0 129.2 jit_solution(12145370908505187316)
XLA Ops:
  0.6 83.5 %block.1 = (bf16[16,24,768]{2,1,0:T(8,128)(2,1)}, bf16[512,768]{1,0:T(8,128)(2,1)}, f32[512,128]{1,0:T(8,128)}, bf16[4,2,2,2,24,768]{5,4,3,2,1,0:T(8,128)(2,1)}) custom-call(bf16[16,24,768]{2,1,0:T(8,128)(2,1)} %tokens.1, f32[7,7,768]{2,1,0:T(8,128)} %dw.1, f32[768]{0:T(1024)} %gain.1, f32[768]{0:T(1024)} %shift.1, bf16[2,2,2,2,48,768]{5,4,3,2,1,0:T(8,128)(2,1)} %bitcast.9, ...), custom_call_target="tpu_custom_call" | custom-call | tf_op jit(solution)/shard_map/block/pallas_call | solution.py:559
  84.1 0.0 copy-start.1
  84.1 41.4 %latents.1 = bf16[512,768]{1,0:T(8,128)(2,1)} custom-call(bf16[512,768]{1,0:T(8,128)(2,1)} %get-tuple-element.7.num_in, f32[512,128]{1,0:T(8,128)} %get-tuple-element.8.stat_in, f32[768]{0:T(1024)} %latent_gain.1), custom_call_target="tpu_custom_call" | custom-call | tf_op jit(solution)/shard_map/latents/pallas_call | solution.py:602
  125.5 0.0 copy-done.1
  125.5 0.0 copy-start
  125.5 2.9 %convolution_convert_fusion = bf16[512,768]{1,0:T(8,128)(2,1)} fusion(bf16[512,768]{1,0:T(8,128)(2,1)} %latents.1, bf16[768,768]{1,0:T(8,128)(2,1)S(1)} %bitcast.13), kind=kOutput, calls=%fused_computation | convolution fusion | flops 604372992 | bytes 2752512 | tf_op jit(solution)/shard_map/dot_general | solution.py:621
  128.4 0.0 copy-done
  128.4 0.8 copy.13
Async XLA Ops:
  84.1 41.4 %copy-start.1 = (bf16[4,2,2,2,24,768]{5,4,3,2,1,0:T(8,128)(2,1)S(1)}, bf16[4,2,2,2,24,768]{5,4,3,2,1,0:T(8,128)(2,1)}, u32[]{:S(2)}) copy-start(bf16[4,2,2,2,24,768]{5,4,3,2,1,0:T(8,128)(2,1)} %get-tuple-element.9) | copy-start | bytes 3538948
  125.5 2.9 %copy-start = (bf16[16,24,768]{2,1,0:T(8,128)(2,1)S(1)}, bf16[16,24,768]{2,1,0:T(8,128)(2,1)}, u32[]{:S(2)}) copy-start(bf16[16,24,768]{2,1,0:T(8,128)(2,1)} %get-tuple-element.12) | copy-start | bytes 1769476

commit v3 on v2

--- a/solution.py
+++ b/solution.py
@@ -425,34 +425,50 @@
             device_id_type=MESH,
         )
 
-    slot = 0
     sent = []
-    base = 0
-    size = latents
+    slots = iter(range(4 * bits + 3 * (cols - 1) + 2 * bits))
+    rest = list(range(1, bits))
+    orders = [[0] + rest, [0] + rest[::-1]]
+    held = [[], []]
     offset = 0
-    bases = []
-    for i in range(bits):
-        half = size // 2
-        mine = base + bit(i) * half
-        theirs = base + (1 - bit(i)) * half
-        src_num, src_stat = (num_in, stat_in) if i == 0 else (num, stat)
-        give = pl.ds(pl.multiple_of(theirs, 16), half)
-        land = pl.ds(offset, half)
+    trips = {}
+
+    def exchange(s, p):
+        nonlocal offset
+        i = orders[s][p]
+        if p == 0:
+            size = latents // 4
+            mine = bit(i) * 2 * size + s * size
+            theirs = (1 - bit(i)) * 2 * size + s * size
+        else:
+            base, whole = held[s][-1]
+            size = whole // 2
+            mine, theirs = base + bit(i) * size, base + (1 - bit(i)) * size
+        src_num, src_stat = (num_in, stat_in) if p == 0 else (num, stat)
+        give = pl.ds(pl.multiple_of(theirs, 16), size)
+        land = pl.ds(offset, size)
         pair = [
-            copy(src_stat.at[give], got_stat.at[land], slot, (partner(i), col)),
-            copy(src_num.at[give], got_num.at[land], slot + 1, (partner(i), col)),
+            copy(src_stat.at[give], got_stat.at[land], next(slots), (partner(i), col)),
+            copy(src_num.at[give], got_num.at[land], next(slots), (partner(i), col)),
         ]
-        slot += 2
         for c in pair:
             c.start()
+        trips[s, p] = (pair, offset)
+        held[s].append((mine, size))
+        offset = offset + size
+
+    def collect(s, p):
+        pair, first = trips[s, p]
         for c in pair:
             c.wait_recv()
-        sent += pair
-        step = min(half, 32)
+        sent.extend(pair)
+        mine, size = held[s][p]
+        src_num, src_stat = (num_in, stat_in) if p == 0 else (num, stat)
+        step = min(size, 32)
 
         def fold(k, carry):
             at = pl.ds(pl.multiple_of(mine + k * step, 16), step)
-            came = pl.ds(pl.multiple_of(offset + k * step, 16), step)
+            came = pl.ds(pl.multiple_of(first + k * step, 16), step)
             new_stat, new_num = merge(
                 [src_stat[at, :], got_stat[came, :]], [src_num[at, :], got_num[came, :]]
             )
@@ -460,21 +476,33 @@
             num[at, :] = new_num.astype(jnp.bfloat16)
             return carry
 
-        lax.fori_loop(0, half // step, fold, 0)
-        bases.append((base, size))
-        base, size, offset = mine, half, offset + half
-
-    share = size // cols
+        lax.fori_loop(0, size // step, fold, 0)
+
+    for s in range(2):
+        exchange(s, 0)
+    for p in range(bits):
+        for s in range(2):
+            collect(s, p)
+            if p + 1 < bits:
+                exchange(s, p + 1)
+
+    share = latents // (rows * cols)
+    side_cols = cols // 2
+
+    def chunk(c):
+        base = jnp.where(
+            c < side_cols, held[0][-1][0] + c * share, held[1][-1][0] + (c - side_cols) * share
+        )
+        return pl.ds(pl.multiple_of(base, 16), share)
+
     arrived = []
     for j in range(1, cols):
         other = (col + cols - j) % cols
-        give = pl.ds(pl.multiple_of(base + other * share, 16), share)
         land = pl.ds(offset + (j - 1) * share, share)
         pair = [
-            copy(stat.at[give], got_stat.at[land], slot, (row, other)),
-            copy(num.at[give], got_num.at[land], slot + 1, (row, other)),
+            copy(stat.at[chunk(other)], got_stat.at[land], next(slots), (row, other)),
+            copy(num.at[chunk(other)], got_num.at[land], next(slots), (row, other)),
         ]
-        slot += 2
         for c in pair:
             c.start()
         sent += pair
@@ -482,7 +510,7 @@
     for pair, _ in arrived:
         for c in pair:
             c.wait_recv()
-    own = pl.ds(pl.multiple_of(base + col * share, 16), share)
+    own = chunk(col)
     final_stat, final_num = merge(
         [stat[own, :]] + [got_stat[land, :] for _, land in arrived],
         [num[own, :]] + [got_num[land, :] for _, land in arrived],
@@ -494,21 +522,26 @@
 
     gather = []
     for j in range(1, cols):
-        c = copy(out.at[own], out.at[own], slot, (row, (col + cols - j) % cols))
-        slot += 1
+        c = copy(out.at[own], out.at[own], next(slots), (row, (col + cols - j) % cols))
         c.start()
         gather.append(c)
     for c in gather:
         c.wait_recv()
     sent += gather
-    for i in reversed(range(bits)):
-        held = pl.ds(pl.multiple_of(base, 16), size)
-        c = copy(out.at[held], out.at[held], slot, (partner(i), col))
-        slot += 1
-        c.start()
-        c.wait_recv()
-        sent.append(c)
-        base, size = bases[i]
+    back = [None, None]
+    for p in reversed(range(bits)):
+        for s in range(2):
+            if back[s] is not None:
+                back[s].wait_recv()
+            base, size = held[s][p]
+            rows_held = pl.ds(pl.multiple_of(base, 16), size)
+            back[s] = copy(
+                out.at[rows_held], out.at[rows_held], next(slots), (partner(orders[s][p]), col)
+            )
+            back[s].start()
+            sent.append(back[s])
+    for s in range(2):
+        back[s].wait_recv()
     for c in sent:
         c.wait_send()
 
@@ -522,6 +555,7 @@
     return (
         mesh_rows >= 2
         and mesh_cols >= 2
+        and mesh_cols % 2 == 0
         and mesh_rows & (mesh_rows - 1) == 0
         and depth % (32 * mesh_rows) == 0
         and w_in.shape[1] % LANES == 0
@@ -598,7 +632,7 @@
         *shards,
         queries,
     )
-    slots = 2 * bits + 3 * (cols - 1) + bits
+    slots = 4 * bits + 3 * (cols - 1) + 2 * bits
     scaled = pl.pallas_call(
         functools.partial(latent_kernel, rows, cols),
         out_shape=jax.ShapeDtypeStruct((latents, depth), bf16),

time: 129 us -> 123 us (0.953)
  Pallas kernels: 125 us -> 119 us
    pallas_call x1, Pallas kernels: 41.4 us -> 35.1 us  [kernel_body(): pl.pallas_call(functools.partial(latent_kernel, rows, cols), out_shape=ja...]
where the time goes in v3:
time: 123 us
  Pallas kernels  119 us (97%)
  matrix products  2.88 us (2%)
    pallas_call x1, Pallas kernels, kernel_body(): pl.pallas_call(functools.partial(block_kernel, rows, cols), out_shape=(ja...  83.5 us
    pallas_call x1, Pallas kernels, kernel_body(): pl.pallas_call(functools.partial(latent_kernel, rows, cols), out_shape=ja...  35.1 us
    dot_general x1, matrix products, kernel_body(): lax.dot_general(scaled, w_turned, (((1,), (1,)), ((), ())), preferred_ele...  2.88 us

profile of v3, /device:TPU:0, one launch (start us, length us, event | category | flops | bytes accessed | tf_op | source)
XLA Modules:
  0.0 122.9 jit_solution(9164391118799954323)
XLA Ops:
  0.6 83.5 %block.1 = (bf16[16,24,768]{2,1,0:T(8,128)(2,1)}, bf16[512,768]{1,0:T(8,128)(2,1)}, f32[512,128]{1,0:T(8,128)}, bf16[4,2,2,2,24,768]{5,4,3,2,1,0:T(8,128)(2,1)}) custom-call(bf16[16,24,768]{2,1,0:T(8,128)(2,1)} %tokens.1, f32[7,7,768]{2,1,0:T(8,128)} %dw.1, f32[768]{0:T(1024)} %gain.1, f32[768]{0:T(1024)} %shift.1, bf16[2,2,2,2,48,768]{5,4,3,2,1,0:T(8,128)(2,1)} %bitcast.9, ...), custom_call_target="tpu_custom_call" | custom-call | tf_op jit(solution)/shard_map/block/pallas_call | solution.py:593
  84.1 0.0 copy-start.1
  84.1 35.1 %latents.1 = bf16[512,768]{1,0:T(8,128)(2,1)} custom-call(bf16[512,768]{1,0:T(8,128)(2,1)} %get-tuple-element.7.num_in, f32[512,128]{1,0:T(8,128)} %get-tuple-element.8.stat_in, f32[768]{0:T(1024)} %latent_gain.1), custom_call_target="tpu_custom_call" | custom-call | tf_op jit(solution)/shard_map/latents/pallas_call | solution.py:636
  119.2 0.0 copy-done.1
  119.2 0.0 copy-start
  119.2 2.9 %convolution_convert_fusion = bf16[512,768]{1,0:T(8,128)(2,1)} fusion(bf16[512,768]{1,0:T(8,128)(2,1)} %latents.1, bf16[768,768]{1,0:T(8,128)(2,1)S(1)} %bitcast.13), kind=kOutput, calls=%fused_computation | convolution fusion | flops 604372992 | bytes 2752512 | tf_op jit(solution)/shard_map/dot_general | solution.py:655
  122.1 0.0 copy-done
  122.1 0.8 copy.13
Async XLA Ops:
  84.1 35.1 %copy-start.1 = (bf16[4,2,2,2,24,768]{5,4,3,2,1,0:T(8,128)(2,1)S(1)}, bf16[4,2,2,2,24,768]{5,4,3,2,1,0:T(8,128)(2,1)}, u32[]{:S(2)}) copy-start(bf16[4,2,2,2,24,768]{5,4,3,2,1,0:T(8,128)(2,1)} %get-tuple-element.9) | copy-start | bytes 3538948
  119.2 2.9 %copy-start = (bf16[16,24,768]{2,1,0:T(8,128)(2,1)S(1)}, bf16[16,24,768]{2,1,0:T(8,128)(2,1)}, u32[]{:S(2)}) copy-start(bf16[16,24,768]{2,1,0:T(8,128)(2,1)} %get-tuple-element.12) | copy-start | bytes 1769476

commit v4 on v3

--- a/solution.py
+++ b/solution.py
@@ -71,6 +71,8 @@
     halo_recv,
     send_sem,
     recv_sem,
+    pass_send,
+    pass_recv,
     local_sem,
 ):
     bits = log2(rows)
@@ -128,20 +130,60 @@
 
     shards = (w_in, w_out, w_kv, w_o)
     fulls = (g_in, g_out, g_kv, wo_out)
-    units = [(w, j) for w in range(4) for j in range(1, cols)]
     own = tuple(coords)
+    units = [(w, k) for w in range(4) for k in range(cols - 1)]
+
+    def rank(c, side, d):
+        both = jnp.minimum(c, cols - 1 - c)
+        return jnp.where(d <= both, 2 * (d - 1) + (0 if side > 0 else 1), d - 1 + both)
+
+    both = jnp.minimum(col, cols - 1 - col)
+    longer = jnp.where(cols - 1 - col > col, 1, -1)
+    sides, gaps, blocks = [], [], []
+    for k in range(cols - 1):
+        paired = k < 2 * both
+        sides.append(jnp.where(paired, 1 - 2 * (k % 2), longer))
+        gaps.append(jnp.where(paired, k // 2 + 1, k - both + 1))
+        blocks.append(col + sides[k] * gaps[k])
+
+    def pass_on(w, k, side):
+        to = col - side
+        block = col if k is None else blocks[k]
+        gap = 1 if k is None else gaps[k] + 1
+        src = shards[w].at[own] if k is None else fulls[w].at[(block,) + own]
+        cond = (to >= 0) & (to < cols)
+        if k is not None:
+            cond = cond & (sides[k] == side)
+        place = (cols - 1 + (0 if side > 0 else 1)) if k is None else k
+        unit = w * (cols - 1) + rank(to, side, gap)
+        return cond, pltpu.make_async_remote_copy(
+            src_ref=src,
+            dst_ref=fulls[w].at[(block,) + own],
+            send_sem=pass_send.at[w * (cols + 1) + place],
+            recv_sem=pass_recv.at[unit],
+            device_id=(row, to),
+            device_id_type=MESH,
+        )
+
+    def each_pass(w, k, act):
+        for side in (1, -1):
+            cond, c = pass_on(w, k, side)
+
+            @pl.when(cond)
+            def _():
+                act(c)
 
     halves = [len(w.shape) - bits - 2 for w in shards]
     ways = bits + (bits - 1) + 1
 
     def unit_copies(u, phase):
-        w, j = units[u]
+        w, k = units[u]
         slot = u * ways
         if phase == 0:
-            target = (row, (col + cols - j) % cols)
-            trips = [(shards[w].at[own], fulls[w].at[(col,) + own], target, slot)]
+            ref = fulls[w].at[(blocks[k],) + own]
+            return [pltpu.make_async_copy(ref, ref, pass_recv.at[u])]
         else:
-            block = (col + j) % cols
+            block = blocks[k]
             split = halves[w] and phase < bits
             trips = []
             for half in range(2 if split else 1):
@@ -168,9 +210,8 @@
             for src, dst, target, at in trips
         ]
 
-    for u in range(len(units)):
-        for c in unit_copies(u, 0):
-            c.start()
+    for w in range(4):
+        each_pass(w, None, lambda c: c.start())
     local = []
     for w in range(4):
         copy = pltpu.make_async_copy(shards[w], fulls[w].at[col], local_sem.at[w])
@@ -190,7 +231,9 @@
             u = t - lag * phase
             if 0 <= u < len(units):
                 for c in unit_copies(u, phase):
-                    c.wait_recv()
+                    c.wait() if phase == 0 else c.wait_recv()
+                if phase == 0:
+                    each_pass(*units[u], lambda c: c.start())
                 if phase < bits:
                     for c in unit_copies(u, phase + 1):
                         c.start()
@@ -296,10 +339,10 @@
     contract(col, True)
     for j in range(1, cols):
         finish_unit(j - 1)
-        expand((col + j) % cols)
+        expand(blocks[j - 1])
     for j in range(1, cols):
         finish_unit(cols - 1 + j - 1)
-        contract((col + j) % cols, False)
+        contract(blocks[j - 1], False)
 
     def close_rows(g, carry):
         base = pad[pl.ds(HALO + g * group, group), pl.ds(EDGE, width), :].reshape(span, depth)
@@ -325,7 +368,7 @@
     project(col)
     for j in range(1, cols):
         finish_unit(2 * (cols - 1) + j - 1)
-        project((col + j) % cols)
+        project(blocks[j - 1])
 
     latents = queries.shape[0]
     scale = 1.0 / math.sqrt(HEAD)
@@ -369,9 +412,12 @@
             halo_copy(i, dr, dc).wait_send()
 
     for u in range(len(units)):
-        for phase in range(bits + 1):
+        each_pass(*units[u], lambda c: c.wait_send())
+        for phase in range(1, bits + 1):
             for c in unit_copies(u, phase):
                 c.wait_send()
+    for w in range(4):
+        each_pass(w, None, lambda c: c.wait_send())
 
 
 def per_head(factors, n):
@@ -618,6 +664,8 @@
             pltpu.SemaphoreType.DMA((8,)),
             pltpu.SemaphoreType.DMA((units * 2 * bits,)),
             pltpu.SemaphoreType.DMA((units * 2 * bits,)),
+            pltpu.SemaphoreType.DMA((4 * (cols + 1),)),
+            pltpu.SemaphoreType.DMA((units,)),
             pltpu.SemaphoreType.DMA((4,)),
         ],
         compiler_params=pltpu.CompilerParams(

time: 123 us -> 118 us (0.959)
  Pallas kernels: 119 us -> 113 us
    pallas_call x1, Pallas kernels: 83.5 us -> 80.5 us  [kernel_body(): pl.pallas_call(functools.partial(block_kernel, rows, cols), out_shape=(ja...]
    pallas_call x1, Pallas kernels: 35.1 us -> 32.9 us  [kernel_body(): pl.pallas_call(functools.partial(latent_kernel, rows, cols), out_shape=ja...]
where the time goes in v4:
time: 118 us
  Pallas kernels  113 us (96%)
  matrix products  2.88 us (2%)
    pallas_call x1, Pallas kernels, kernel_body(): pl.pallas_call(functools.partial(block_kernel, rows, cols), out_shape=(ja...  80.5 us
    pallas_call x1, Pallas kernels, kernel_body(): pl.pallas_call(functools.partial(latent_kernel, rows, cols), out_shape=ja...  32.9 us
    dot_general x1, matrix products, kernel_body(): lax.dot_general(scaled, w_turned, (((1,), (1,)), ((), ())), preferred_ele...  2.88 us

profile of v4, /device:TPU:0, one launch (start us, length us, event | category | flops | bytes accessed | tf_op | source)
XLA Modules:
  0.0 117.9 jit_solution(1034827102953835493)
XLA Ops:
  0.6 80.5 %block.1 = (bf16[16,24,768]{2,1,0:T(8,128)(2,1)}, bf16[512,768]{1,0:T(8,128)(2,1)}, f32[512,128]{1,0:T(8,128)}, bf16[4,2,2,2,24,768]{5,4,3,2,1,0:T(8,128)(2,1)}) custom-call(bf16[16,24,768]{2,1,0:T(8,128)(2,1)} %tokens.1, f32[7,7,768]{2,1,0:T(8,128)} %dw.1, f32[768]{0:T(1024)} %gain.1, f32[768]{0:T(1024)} %shift.1, bf16[2,2,2,2,48,768]{5,4,3,2,1,0:T(8,128)(2,1)} %bitcast.9, ...), custom_call_target="tpu_custom_call" | custom-call | tf_op jit(solution)/shard_map/block/pallas_call | solution.py:639
  81.2 0.0 copy-start.1
  81.2 32.9 %latents.1 = bf16[512,768]{1,0:T(8,128)(2,1)} custom-call(bf16[512,768]{1,0:T(8,128)(2,1)} %get-tuple-element.7.num_in, f32[512,128]{1,0:T(8,128)} %get-tuple-element.8.stat_in, f32[768]{0:T(1024)} %latent_gain.1), custom_call_target="tpu_custom_call" | custom-call | tf_op jit(solution)/shard_map/latents/pallas_call | solution.py:684
  114.1 0.0 copy-done.1
  114.1 0.0 copy-start
  114.2 2.9 %convolution_convert_fusion = bf16[512,768]{1,0:T(8,128)(2,1)} fusion(bf16[512,768]{1,0:T(8,128)(2,1)} %latents.1, bf16[768,768]{1,0:T(8,128)(2,1)S(1)} %bitcast.13), kind=kOutput, calls=%fused_computation | convolution fusion | flops 604372992 | bytes 2752512 | tf_op jit(solution)/shard_map/dot_general | solution.py:703
  117.0 0.0 copy-done
  117.0 0.8 copy.13
Async XLA Ops:
  81.2 33.0 %copy-start.1 = (bf16[4,2,2,2,24,768]{5,4,3,2,1,0:T(8,128)(2,1)S(1)}, bf16[4,2,2,2,24,768]{5,4,3,2,1,0:T(8,128)(2,1)}, u32[]{:S(2)}) copy-start(bf16[4,2,2,2,24,768]{5,4,3,2,1,0:T(8,128)(2,1)} %get-tuple-element.9) | copy-start | bytes 3538948
  114.1 2.9 %copy-start = (bf16[16,24,768]{2,1,0:T(8,128)(2,1)S(1)}, bf16[16,24,768]{2,1,0:T(8,128)(2,1)}, u32[]{:S(2)}) copy-start(bf16[16,24,768]{2,1,0:T(8,128)(2,1)} %get-tuple-element.12) | copy-start | bytes 1769476
